TPU v7x, 128 devices: a whole 4x4x4 slice. The times are simulated.
128 devices in a mesh: row: 16 (over z_hi, y, core), col: 8 (over x, z_lo).
Axes of the slice: x: 4, y: 4, z: 4 (z_hi: 2, z_lo: 2; z = z_hi * 2 + z_lo), core: 2. Of those that a mesh axis runs over, the one named last changes fastest.
Arguments:
- word_topic: bfloat16 [131072, 128], P(('row', 'col')), may hold values from 0.25 to 4
- topic_weight: float32 [128], replicated, may hold values from 0.1 to 10
- tile_blocks: int32 [16, 8, 64, 2], P('row', 'col'), may hold values from 0 to 63, as said below
- tile_live: int32 [16, 8], P('row', 'col'), may hold values from 16 to 64, as said below
- pair_counts: int32 [16, 8, 64, 256, 256], P('row', 'col'), may hold values from 0 to 63
Outputs:
- next_word_topic: bfloat16 [131072, 128], P(('row', 'col'))
- next_topic_weight: float32 [128], replicated
Inputs may be any that keep to these rules, and one draw needn't show every extreme that they name: `tile_blocks`: each entry pair is (a word block among the device's 32 blocks of first words, a word block among its 64 blocks of second words); the slots of one device name distinct tiles. `tile_live`: slots at or beyond a device's count hold no tile; some device fills all slots.
All inputs are finite; a program needn't handle non-finite values.
Results may differ from a plain program's by a relative error of at most 0.0049.
Values may be sent and summed in bfloat16 or wider, within the bound.
No kernel may reach another device: no remote copies, remote signals or barrier semaphores. Data moves between devices by JAX's collectives and lax.ppermute only.
A program may use at most 128 MiB of HBM per device.

v0:
```python
from functools import partial
import jax
import jax.numpy as jnp
from jax import lax
from jax.sharding import PartitionSpec as P

V = 131072
K = 128
BLK = 256
ITERS = 2


def group_step(
    left_blocks, right_blocks, blocks, tiles_all, live, want_row, want_col, group, carry
):
    tile_group = 8
    start = group * tile_group
    row_ids = lax.dynamic_slice_in_dim(blocks[:, 0], start, tile_group)
    col_ids = lax.dynamic_slice_in_dim(blocks[:, 1], start, tile_group)
    tiles = lax.dynamic_slice_in_dim(tiles_all, start, tile_group, 0)
    alive = start + jnp.arange(tile_group, dtype=jnp.int32) < live
    left = left_blocks[row_ids]
    right = right_blocks[col_ids]
    denoms = jnp.einsum("gak,gbk->gab", left, right, preferred_element_type=jnp.float32)
    ratio = jnp.where(alive[:, None, None], tiles.astype(jnp.float32) / denoms, 0.0).astype(
        jnp.bfloat16
    )
    results = []
    place = 0
    row_part = jnp.einsum("gab,gbk->gak", ratio, right, preferred_element_type=jnp.float32)
    results.append(carry[place].at[row_ids].add(row_part))
    place = place + 1
    col_part = jnp.einsum("gab,gak->gbk", ratio, left, preferred_element_type=jnp.float32)
    results.append(carry[place].at[col_ids].add(col_part))
    return tuple(results)


def sweep(left_blocks, right_blocks, blocks, tiles_all, live):
    starts = []
    starts.append(jnp.zeros(left_blocks.shape, jnp.float32))
    starts.append(jnp.zeros(right_blocks.shape, jnp.float32))
    stepper = partial(group_step, left_blocks, right_blocks, blocks, tiles_all, live, True, True)
    turns = (live + 7) // 8
    return lax.fori_loop(0, turns, stepper, tuple(starts))


def local(word_topic, topic_weight, tile_blocks, tile_live, pair_counts):
    blocks = tile_blocks[0, 0]
    live = tile_live[0, 0]
    tiles_all = pair_counts[0, 0]
    weights = word_topic
    shares = topic_weight
    for step in range(ITERS):
        row_phi = lax.all_gather(weights, "col", axis=0, tiled=True)
        col_phi = lax.all_gather(weights, "row", axis=0, tiled=True)
        scaled = (row_phi.astype(jnp.float32) * shares).astype(jnp.bfloat16)
        left_blocks = scaled.reshape(-1, BLK, K)
        right_blocks = col_phi.reshape(-1, BLK, K)
        row_acc, col_acc = sweep(left_blocks, right_blocks, blocks, tiles_all, live)
        row_terms = row_acc.reshape(-1, K)
        col_terms = col_acc.reshape(-1, K)
        row_sum = lax.psum_scatter(row_terms, "col", scatter_dimension=0, tiled=True)
        col_sum = lax.psum_scatter(col_terms, "row", scatter_dimension=0, tiled=True)
        expected = weights.astype(jnp.float32) * (shares * row_sum + col_sum)
        totals = lax.psum(jnp.sum(expected, axis=0), ("row", "col"))
        weights = (V * expected / totals).astype(jnp.bfloat16)
        shares = K * totals / jnp.sum(totals)
    return (weights, shares)


def solution(mesh):
    in_specs = (
        P(("row", "col"), None),
        P(),
        P("row", "col", None, None),
        P("row", "col"),
        P("row", "col", None, None, None),
    )
    out_specs = (P(("row", "col"), None), P())
    return jax.shard_map(local, mesh=mesh, in_specs=in_specs, out_specs=out_specs, check_vma=False)
```

profile of v0, /device:TPU:1, one launch (start us, length us, event | category | flops | bytes accessed | tf_op | source)
XLA Modules:
  0.0 1029.4 jit_solution(16607636807630387287)
XLA Ops:
  9.4 52.8 %all-gather.5.cloned.1.call-done = bf16[8192,128]{1,0:T(8,128)(2,1)} async-done(((bf16[1024,128]{1,0:T(8,128)(2,1)}), bf16[8192,128]{1,0:T(8,128)(2,1)}) %all-gather.5.cloned.1.call-update) | async-done | bytes 2097168 | tf_op jit(solution)/shard_map/all_gather | solution.py:54
  62.1 3.3 multiply_convert_fusion.1
  65.5 57.8 %all-gather.7.cloned.1.call-done = bf16[16384,128]{1,0:T(8,128)(2,1)} async-done(((bf16[1024,128]{1,0:T(8,128)(2,1)}), bf16[16384,128]{1,0:T(8,128)(2,1)}) %all-gather.7.cloned.1.call-update) | async-done | bytes 4194320 | tf_op jit(solution)/shard_map/all_gather | solution.py:55
  123.3 4.2 broadcast.60.clone
  130.0 108.6 %while.24 = (s32[]{:T(128)}, f32[32,256,128]{2,1,0:T(8,128)}, f32[64,256,128]{2,1,0:T(8,128)}, s32[]{:T(128)}, s32[64,2]{0,1:T(2,128)S(1)}, /*index=5*/s32[]{:T(...) while((s32[]{:T(128)}, f32[32,256,128]{2,1,0:T(8,128)}, ...), condition=%wide.region_3.4_spmd, body=%wide.region_0.3_spmd.sunk | while | flops 405276736 | bytes 17835532 | solution.py:44
  138.4 3.4 scatter_fusion.1
  142.3 3.3 scatter_fusion
  154.1 3.3 scatter_fusion.1
  173.3 3.3 scatter_fusion
  185.0 3.4 scatter_fusion.1
  216.0 3.4 scatter_fusion.1
  231.5 3.4 scatter_fusion.1
  235.3 3.4 scatter_fusion
  239.3 103.5 %reduce-scatter.5.cloned.1.call-done = f32[1024,128]{1,0:T(8,128)} async-done(((f32[8192,128]{1,0:T(8,128)}), f32[1024,128]{1,0:T(8,128)}) %reduce-scatter.5.cloned.1.call-update) | async-done | bytes 524304 | tf_op jit(solution)/shard_map/reduce_scatter | solution.py:62
  342.8 106.7 %reduce-scatter.7.cloned.1.call-done = f32[1024,128]{1,0:T(8,128)} async-done(((f32[16384,128]{1,0:T(8,128)}), f32[1024,128]{1,0:T(8,128)}) %reduce-scatter.7.cloned.1.call-update) | async-done | bytes 524304 | tf_op jit(solution)/shard_map/reduce_scatter | solution.py:63
  450.9 65.3 %psum.14 = f32[128]{0:T(128)S(1)} all-reduce(f32[128]{0:T(128)S(1)} %fusion.4), channel_id=1, replica_groups=mesh['row'=16,'col'=8] {'row','col'}, use_global_device_ids=true, to_apply=%region_7.8 | all-reduce | flops 128 | bytes 1024 | tf_op jit(solution)/shard_map/psum | solution.py:65
  520.1 43.9 %all-gather.9.cloned.1.call-done = bf16[8192,128]{1,0:T(8,128)(2,1)} async-done(((bf16[1024,128]{1,0:T(8,128)(2,1)}), bf16[8192,128]{1,0:T(8,128)(2,1)}) %all-gather.9.cloned.1.call-update) | async-done | bytes 2097168 | tf_op jit(solution)/shard_map/all_gather | solution.py:54
  564.1 3.3 multiply_convert_fusion
  567.4 58.3 %all-gather.11.cloned.1.call-done = bf16[16384,128]{1,0:T(8,128)(2,1)} async-done(((bf16[1024,128]{1,0:T(8,128)(2,1)}), bf16[16384,128]{1,0:T(8,128)(2,1)}) %all-gather.11.cloned.1.call-update) | async-done | bytes 4194320 | tf_op jit(solution)/shard_map/all_gather | solution.py:55
  625.7 4.2 broadcast.60
  632.4 108.6 %while.25 = (s32[]{:T(128)}, f32[32,256,128]{2,1,0:T(8,128)}, f32[64,256,128]{2,1,0:T(8,128)}, s32[]{:T(128)}, s32[64,2]{0,1:T(2,128)S(1)}, /*index=5*/s32[]{:T(...) while((s32[]{:T(128)}, f32[32,256,128]{2,1,0:T(8,128)}, ...), condition=%wide.region_12.13_spmd, body=%wide.region_9.12_spmd.sunk | while | flops 405276736 | bytes 17835532 | solution.py:44
  640.8 3.4 scatter_fusion.3
  644.6 3.3 scatter_fusion.2
  656.4 3.3 scatter_fusion.3
  675.6 3.3 scatter_fusion.2
  687.4 3.4 scatter_fusion.3
  718.4 3.4 scatter_fusion.3
  733.9 3.4 scatter_fusion.3
  737.7 3.4 scatter_fusion.2
  741.8 103.4 %reduce-scatter.9.cloned.1.call-done = f32[1024,128]{1,0:T(8,128)} async-done(((f32[8192,128]{1,0:T(8,128)}), f32[1024,128]{1,0:T(8,128)}) %reduce-scatter.9.cloned.1.call-update) | async-done | bytes 524304 | tf_op jit(solution)/shard_map/reduce_scatter | solution.py:62
  845.2 106.7 %reduce-scatter.11.cloned.1.call-done = f32[1024,128]{1,0:T(8,128)} async-done(((f32[16384,128]{1,0:T(8,128)}), f32[1024,128]{1,0:T(8,128)}) %reduce-scatter.11.cloned.1.call-update) | async-done | bytes 524304 | tf_op jit(solution)/shard_map/reduce_scatter | solution.py:63
  953.2 65.5 %psum.15 = f32[128]{0:T(128)S(1)} all-reduce(f32[128]{0:T(128)S(1)} %fusion.5), channel_id=1, replica_groups=mesh['row'=16,'col'=8] {'row','col'}, use_global_device_ids=true, to_apply=%region_16.17 | all-reduce | flops 128 | bytes 1024 | tf_op jit(solution)/shard_map/psum | solution.py:65
  (186 shorter events, 180.9 us)
Async XLA Ops:
  7.2 55.0 %all-gather.5.cloned.1.call-start = ((), (), s32[]{:S(2)}) async-start(), calls=%async_computation.4 | async-start | bytes 2359296 | tf_op jit(solution)/shard_map/all_gather | solution.py:54
  7.9 115.4 %all-gather.7.cloned.1.call-start = ((), (), s32[]{:S(2)}) async-start(), calls=%async_computation.5 | async-start | bytes 4456448 | tf_op jit(solution)/shard_map/all_gather | solution.py:55
  8.6 334.2 %reduce-scatter.5.cloned.1.call-start = ((), (), s32[]{:S(2)}) async-start(), calls=%async_computation.6 | async-start | bytes 4718592 | tf_op jit(solution)/shard_map/reduce_scatter | solution.py:62
  127.6 2.5 copy-start.2
  238.7 210.9 %reduce-scatter.7.cloned.1.call-start = ((), (), s32[]{:S(2)}) async-start(), calls=%async_computation.7 | async-start | bytes 8912896 | tf_op jit(solution)/shard_map/reduce_scatter | solution.py:63
  238.7 210.8 %copy-start.1 = (bf16[1024,128]{1,0:T(8,128)(2,1)S(1)}, bf16[1024,128]{1,0:T(8,128)(2,1)}, u32[]{:S(2)}) copy-start(bf16[1024,128]{1,0:T(8,128)(2,1)} %param.9) | copy-start | bytes 786436
  238.7 210.8 %copy-start.3 = (f32[128]{0:T(128)S(1)}, f32[128]{0:T(128)}, u32[]{:S(2)}) copy-start(f32[128]{0:T(128)} %param.10) | copy-start | bytes 1540
  239.3 324.8 %all-gather.9.cloned.1.call-start = ((), (), s32[]{:S(2)}) async-start(), calls=%async_computation.8 | async-start | bytes 2359296 | tf_op jit(solution)/shard_map/all_gather | solution.py:54
  518.2 107.5 %all-gather.11.cloned.1.call-start = ((), (), s32[]{:S(2)}) async-start(), calls=%async_computation.9 | async-start | bytes 4456448 | tf_op jit(solution)/shard_map/all_gather | solution.py:55
  518.8 326.4 %reduce-scatter.9.cloned.1.call-start = ((), (), s32[]{:S(2)}) async-start(), calls=%async_computation.10 | async-start | bytes 4718592 | tf_op jit(solution)/shard_map/reduce_scatter | solution.py:62
  741.0 210.8 %reduce-scatter.11.cloned.1.call-start = ((), (), s32[]{:S(2)}) async-start(), calls=%async_computation.11 | async-start | bytes 8912896 | tf_op jit(solution)/shard_map/reduce_scatter | solution.py:63
  741.1 210.8 %copy-start = (bf16[1024,128]{1,0:T(8,128)(2,1)S(1)}, bf16[1024,128]{1,0:T(8,128)(2,1)}, u32[]{:S(2)}) copy-start(bf16[1024,128]{1,0:T(8,128)(2,1)} %divide_convert_fusion.1) | copy-start | bytes 786436
Sparse Core Ops, SparseCore 0:
  9.6 52.4 all-gather.4
  64.6 58.7 all-gather.6
  238.8 103.9 reduce-scatter.4
  347.0 102.4 reduce-scatter.6
  518.3 45.6 all-gather.8
  566.9 58.7 all-gather.10
  741.2 103.9 reduce-scatter.8
  849.5 102.2 reduce-scatter.10
where the time goes:
time: 1030 us
  waiting for transfers between devices  636 us (62%)
  blocking collectives  131 us (13%)
  other arithmetic  120 us (12%)
  local copies, waits for them, and re-layouts  84.5 us (8%)
  matrix products  41.8 us (4%)
  between operations  14.8 us (1%)
    reduce_scatter x2, waiting for transfers between devices, local(): lax.psum_scatter(col_terms, 'row', scatter_dimension=0, tiled=True)  213 us
    reduce_scatter x2, waiting for transfers between devices, local(): lax.psum_scatter(row_terms, 'col', scatter_dimension=0, tiled=True)  207 us
    psum x2, blocking collectives, local(): totals = lax.psum(jnp.sum(expected, axis=0), ('row', 'col'))  131 us
    all_gather x2, waiting for transfers between devices, local(): col_phi = lax.all_gather(weights, 'row', axis=0, tiled=True)  116 us
    all_gather x2, waiting for transfers between devices, local(): row_phi = lax.all_gather(weights, 'col', axis=0, tiled=True)  96.7 us
    scatter-add x14, other arithmetic, group_step(): results.append(carry[place].at[col_ids].add(col_part))  46.9 us
    scatter-add x14, other arithmetic, group_step(): results.append(carry[place].at[row_ids].add(row_part))  46.4 us
    gather x14, local copies, waits for them, and re-layouts, group_step(): right = right_blocks[col_ids]  39.7 us
  transfers between devices with their start and end apart: 8, of which 8 were waited for; matrix products, arithmetic and copies ran while one was open for 1% of the time, Pallas kernels for 0%

commit v1 on v0

--- a/solution.py
+++ b/solution.py
@@ -62,7 +62,7 @@
         row_sum = lax.psum_scatter(row_terms, "col", scatter_dimension=0, tiled=True)
         col_sum = lax.psum_scatter(col_terms, "row", scatter_dimension=0, tiled=True)
         expected = weights.astype(jnp.float32) * (shares * row_sum + col_sum)
-        totals = lax.psum(jnp.sum(expected, axis=0), ("row", "col"))
+        totals = jnp.sum(lax.all_gather(jnp.sum(expected, axis=0), ("row", "col")), axis=0)
         weights = (V * expected / totals).astype(jnp.bfloat16)
         shares = K * totals / jnp.sum(totals)
     return (weights, shares)

time: 1030 us -> 1520 us (1.48)
  blocking collectives: 131 us -> 592 us
    all_gather x0 -> x2, blocking collectives: none -> 592 us  [local(): lax.all_gather(jnp.sum(expected, axis=0), ('row', 'col'))]
    psum x2 -> x0, blocking collectives: 131 us -> none  [local(): totals = lax.psum(jnp.sum(expected, axis=0), ('row', 'col'))]
  transfers between devices with their start and end apart: 8 -> 8, of which waited for: 8 -> 8; matrix products, arithmetic and copies ran while one was open for 1% -> 0% of each run, Pallas kernels for 0% -> 0%
where the time goes in v1:
time: 1520 us; the launch traced here: 1500 us
  waiting for transfers between devices  650 us (43%)
  blocking collectives  592 us (39%)
  other arithmetic  120 us (8%)
  local copies, waits for them, and re-layouts  84.5 us (6%)
  matrix products  41.8 us (3%)
    all_gather x2, blocking collectives, local(): lax.all_gather(jnp.sum(expected, axis=0), ('row', 'col'))  592 us
    reduce_scatter x2, waiting for transfers between devices, local(): lax.psum_scatter(col_terms, 'row', scatter_dimension=0, tiled=True)  213 us
    reduce_scatter x2, waiting for transfers between devices, local(): lax.psum_scatter(row_terms, 'col', scatter_dimension=0, tiled=True)  207 us
    all_gather x2, waiting for transfers between devices, local(): col_phi = lax.all_gather(weights, 'row', axis=0, tiled=True)  116 us
    all_gather x2, waiting for transfers between devices, local(): row_phi = lax.all_gather(weights, 'col', axis=0, tiled=True)  110 us
    scatter-add x14, other arithmetic, group_step(): results.append(carry[place].at[col_ids].add(col_part))  46.9 us
    scatter-add x14, other arithmetic, group_step(): results.append(carry[place].at[row_ids].add(row_part))  46.4 us
    gather x14, local copies, waits for them, and re-layouts, group_step(): right = right_blocks[col_ids]  39.7 us
  transfers between devices with their start and end apart: 8, of which 8 were waited for; matrix products, arithmetic and copies ran while one was open for 0% of the time, Pallas kernels for 0%

profile of v1, /device:TPU:1, one launch (start us, length us, event | category | flops | bytes accessed | tf_op | source)
XLA Modules:
  0.0 1504.5 jit_solution(14512551274146057220)
XLA Ops:
  9.4 52.8 %all-gather.9.cloned.1.call-done = bf16[8192,128]{1,0:T(8,128)(2,1)} async-done(((bf16[1024,128]{1,0:T(8,128)(2,1)}), bf16[8192,128]{1,0:T(8,128)(2,1)}) %all-gather.9.cloned.1.call-update) | async-done | bytes 2097168 | tf_op jit(solution)/shard_map/all_gather | solution.py:54
  62.1 3.3 multiply_convert_fusion.1
  65.5 57.8 %all-gather.11.cloned.1.call-done = bf16[16384,128]{1,0:T(8,128)(2,1)} async-done(((bf16[1024,128]{1,0:T(8,128)(2,1)}), bf16[16384,128]{1,0:T(8,128)(2,1)}) %all-gather.11.cloned.1.call-update) | async-done | bytes 4194320 | tf_op jit(solution)/shard_map/all_gather | solution.py:55
  123.3 4.2 broadcast.67.clone
  130.0 108.6 %while.24 = (s32[]{:T(128)}, f32[32,256,128]{2,1,0:T(8,128)}, f32[64,256,128]{2,1,0:T(8,128)}, s32[]{:T(128)}, s32[64,2]{0,1:T(2,128)S(1)}, /*index=5*/s32[]{:T(...) while((s32[]{:T(128)}, f32[32,256,128]{2,1,0:T(8,128)}, ...), condition=%wide.region_3.4_spmd, body=%wide.region_0.3_spmd.sunk | while | flops 405276736 | bytes 17835532 | solution.py:44
  138.4 3.4 scatter_fusion.1
  142.3 3.3 scatter_fusion
  154.1 3.3 scatter_fusion.1
  173.3 3.3 scatter_fusion
  185.0 3.4 scatter_fusion.1
  216.0 3.4 scatter_fusion.1
  231.5 3.4 scatter_fusion.1
  235.3 3.4 scatter_fusion
  239.3 103.5 %reduce-scatter.5.cloned.1.call-done = f32[1024,128]{1,0:T(8,128)} async-done(((f32[8192,128]{1,0:T(8,128)}), f32[1024,128]{1,0:T(8,128)}) %reduce-scatter.5.cloned.1.call-update) | async-done | bytes 524304 | tf_op jit(solution)/shard_map/reduce_scatter | solution.py:62
  342.8 106.7 %reduce-scatter.7.cloned.1.call-done = f32[1024,128]{1,0:T(8,128)} async-done(((f32[16384,128]{1,0:T(8,128)}), f32[1024,128]{1,0:T(8,128)}) %reduce-scatter.7.cloned.1.call-update) | async-done | bytes 524304 | tf_op jit(solution)/shard_map/reduce_scatter | solution.py:63
  450.9 296.0 %all-gather.2 = f32[128,1,128]{2,1,0:T(1,128)S(1)} all-gather(f32[1,1,128]{2,1,0:T(1,128)S(1)} %bitcast.69), channel_id=2, replica_groups=mesh['row'=16,'col'=8] {'row','col'}, dimensions={0}, use_global_device_ids=true | all-gather | bytes 66048 | tf_op jit(solution)/shard_map/all_gather | solution.py:65
  751.0 57.3 %all-gather.13.cloned.1.call-done = bf16[8192,128]{1,0:T(8,128)(2,1)} async-done(((bf16[1024,128]{1,0:T(8,128)(2,1)}), bf16[8192,128]{1,0:T(8,128)(2,1)}) %all-gather.13.cloned.1.call-update) | async-done | bytes 2097168 | tf_op jit(solution)/shard_map/all_gather | solution.py:54
  808.3 3.3 multiply_convert_fusion
  811.7 58.3 %all-gather.15.cloned.1.call-done = bf16[16384,128]{1,0:T(8,128)(2,1)} async-done(((bf16[1024,128]{1,0:T(8,128)(2,1)}), bf16[16384,128]{1,0:T(8,128)(2,1)}) %all-gather.15.cloned.1.call-update) | async-done | bytes 4194320 | tf_op jit(solution)/shard_map/all_gather | solution.py:55
  870.0 4.2 broadcast.67
  876.7 108.6 %while.25 = (s32[]{:T(128)}, f32[32,256,128]{2,1,0:T(8,128)}, f32[64,256,128]{2,1,0:T(8,128)}, s32[]{:T(128)}, s32[64,2]{0,1:T(2,128)S(1)}, /*index=5*/s32[]{:T(...) while((s32[]{:T(128)}, f32[32,256,128]{2,1,0:T(8,128)}, ...), condition=%wide.region_12.13_spmd, body=%wide.region_9.12_spmd.sunk | while | flops 405276736 | bytes 17835532 | solution.py:44
  885.1 3.4 scatter_fusion.3
  888.9 3.3 scatter_fusion.2
  900.7 3.3 scatter_fusion.3
  919.9 3.3 scatter_fusion.2
  931.7 3.4 scatter_fusion.3
  962.6 3.4 scatter_fusion.3
  978.1 3.4 scatter_fusion.3
  982.0 3.4 scatter_fusion.2
  986.1 103.4 %reduce-scatter.9.cloned.1.call-done = f32[1024,128]{1,0:T(8,128)} async-done(((f32[8192,128]{1,0:T(8,128)}), f32[1024,128]{1,0:T(8,128)}) %reduce-scatter.9.cloned.1.call-update) | async-done | bytes 524304 | tf_op jit(solution)/shard_map/reduce_scatter | solution.py:62
  1089.5 106.6 %reduce-scatter.11.cloned.1.call-done = f32[1024,128]{1,0:T(8,128)} async-done(((f32[16384,128]{1,0:T(8,128)}), f32[1024,128]{1,0:T(8,128)}) %reduce-scatter.11.cloned.1.call-update) | async-done | bytes 524304 | tf_op jit(solution)/shard_map/reduce_scatter | solution.py:63
  1197.5 296.2 %all-gather.3 = f32[128,1,128]{2,1,0:T(1,128)S(1)} all-gather(f32[1,1,128]{2,1,0:T(1,128)S(1)} %bitcast.70), channel_id=3, replica_groups=mesh['row'=16,'col'=8] {'row','col'}, dimensions={0}, use_global_device_ids=true | all-gather | bytes 66048 | tf_op jit(solution)/shard_map/all_gather | solution.py:65
  (186 shorter events, 181.1 us)
Async XLA Ops:
  7.2 55.0 %all-gather.9.cloned.1.call-start = ((), (), s32[]{:S(2)}) async-start(), calls=%async_computation.4 | async-start | bytes 2359296 | tf_op jit(solution)/shard_map/all_gather | solution.py:54
  7.9 115.4 %all-gather.11.cloned.1.call-start = ((), (), s32[]{:S(2)}) async-start(), calls=%async_computation.5 | async-start | bytes 4456448 | tf_op jit(solution)/shard_map/all_gather | solution.py:55
  8.6 334.2 %reduce-scatter.5.cloned.1.call-start = ((), (), s32[]{:S(2)}) async-start(), calls=%async_computation.6 | async-start | bytes 4718592 | tf_op jit(solution)/shard_map/reduce_scatter | solution.py:62
  127.6 2.5 copy-start.2
  238.7 210.9 %reduce-scatter.7.cloned.1.call-start = ((), (), s32[]{:S(2)}) async-start(), calls=%async_computation.7 | async-start | bytes 8912896 | tf_op jit(solution)/shard_map/reduce_scatter | solution.py:63
  238.7 210.8 %copy-start.1 = (bf16[1024,128]{1,0:T(8,128)(2,1)S(1)}, bf16[1024,128]{1,0:T(8,128)(2,1)}, u32[]{:S(2)}) copy-start(bf16[1024,128]{1,0:T(8,128)(2,1)} %param.9) | copy-start | bytes 786436
  238.7 210.8 %copy-start.3 = (f32[128]{0:T(128)S(1)}, f32[128]{0:T(128)}, u32[]{:S(2)}) copy-start(f32[128]{0:T(128)} %param.10) | copy-start | bytes 1540
  239.3 569.1 %all-gather.13.cloned.1.call-start = ((), (), s32[]{:S(2)}) async-start(), calls=%async_computation.8 | async-start | bytes 2359296 | tf_op jit(solution)/shard_map/all_gather | solution.py:54
  749.7 120.2 %all-gather.15.cloned.1.call-start = ((), (), s32[]{:S(2)}) async-start(), calls=%async_computation.9 | async-start | bytes 4456448 | tf_op jit(solution)/shard_map/all_gather | solution.py:55
  750.3 339.2 %reduce-scatter.9.cloned.1.call-start = ((), (), s32[]{:S(2)}) async-start(), calls=%async_computation.10 | async-start | bytes 4718592 | tf_op jit(solution)/shard_map/reduce_scatter | solution.py:62
  985.3 210.8 %reduce-scatter.11.cloned.1.call-start = ((), (), s32[]{:S(2)}) async-start(), calls=%async_computation.11 | async-start | bytes 8912896 | tf_op jit(solution)/shard_map/reduce_scatter | solution.py:63
  985.4 210.7 %copy-start = (bf16[1024,128]{1,0:T(8,128)(2,1)S(1)}, bf16[1024,128]{1,0:T(8,128)(2,1)}, u32[]{:S(2)}) copy-start(bf16[1024,128]{1,0:T(8,128)(2,1)} %divide_convert_fusion.1) | copy-start | bytes 786436
Sparse Core Ops, SparseCore 0:
  9.6 52.4 all-gather.8
  64.6 58.7 all-gather.10
  238.8 103.9 reduce-scatter.4
  347.0 102.4 reduce-scatter.6
  749.9 58.4 all-gather.12
  811.2 58.7 all-gather.14
  985.4 103.9 reduce-scatter.8
  1093.8 102.2 reduce-scatter.10
